TPU v7x, 128 devices: a whole 4x4x4 slice. The times are simulated.
128 devices in a mesh: tx: 8 (over y, core), ty: 16 (over z, x).
Axes of the slice: x: 4, y: 4, z: 4, core: 2. Of those that a mesh axis runs over, the one named last changes fastest.
Arguments:
- increment: float32 [32, 640, 3072], P(None, 'ty', 'tx'), may hold values from -6 to 6
- vert_rate: float32 [2, 16], replicated, may hold values from 0.05 to 0.8
- zonal_rate: float32 [16, 32], replicated, may hold values from 0.003 to 0.12
- merid_rate: float32 [16, 32], replicated, may hold values from 0.02 to 0.12
- lat_band: int32 [640], replicated, may hold values from 0 to 15, never falling along the last dimension, each value on 1 to 80 neighbouring positions
- slab_owner: int32 [32], replicated, may hold values from 0 to 7, as said below
Outputs:
- covariance_product: float32 [32, 640, 3072], P(None, 'ty', 'tx')
- filtered_slabs: float32 [64, 640, 3072], P('tx', 'ty')
Inputs may be any that keep to these rules, and one draw needn't show every extreme that they name: lat_band never falls along y and every band appears. `slab_owner`: each index of tx owns at most 8 slabs, and some index owns exactly 8.
All inputs are finite; a program needn't handle non-finite values.
Results may differ from a plain program's by a relative error of at most 0.0003.
Values sent between devices are 32-bit elements; how exact they have to be, the bound alone decides.
A program may use at most 128 MiB of HBM per device.

v0:
```python
import jax
import jax.numpy as jnp
from jax import lax
from jax.sharding import PartitionSpec as P

LEV = 16
VAR = 2
NBANDS = 16
HIGHEST_PRECISION = lax.Precision.HIGHEST


def chain_matrices(log_decay, gains):
    length = log_decay.shape[-1]
    inclusive = jnp.cumsum(log_decay, axis=-1)
    exclusive = inclusive - log_decay
    index = jnp.arange(length)
    lower = index[:, None] >= index[None, :]
    upper = index[:, None] <= index[None, :]
    fdiff = inclusive[..., :, None] - inclusive[..., None, :]
    forward = jnp.where(lower, jnp.exp(jnp.where(lower, fdiff, 0.0)), 0.0) * gains[..., None, :]
    bdiff = exclusive[..., None, :] - exclusive[..., :, None]
    backward = jnp.where(upper, jnp.exp(jnp.where(upper, bdiff, 0.0)), 0.0) * gains[..., None, :]
    return (forward, backward)


def gain_of(rates):
    return jnp.sqrt(rates * (2.0 - rates))


def vertical_apply(vert_matrix, values):
    slabs, tile_rows, tile_cols = values.shape
    stacked = values.reshape(VAR, LEV, tile_rows * tile_cols)
    result = jnp.einsum("vlk,vkn->vln", vert_matrix, stacked, precision=HIGHEST_PRECISION)
    return result.reshape(slabs, tile_rows, tile_cols)


def affine_combine(first, second):
    return (first[0] * second[0], second[0] * first[1] + second[1])


def carry_blocks(block_decay, ends):
    scale = jnp.broadcast_to(block_decay, ends.shape)
    inclusive = lax.associative_scan(affine_combine, (scale, ends), axis=2)[1]
    return jnp.concatenate([jnp.zeros_like(inclusive[..., :1]), inclusive[..., :-1]], axis=2)


def carry_row_blocks(block_decay, ends):
    scale = jnp.broadcast_to(block_decay[..., None], ends.shape)
    inclusive = lax.associative_scan(affine_combine, (scale, ends), axis=1)[1]
    return jnp.concatenate([jnp.zeros_like(inclusive[:, :1]), inclusive[:, :-1]], axis=1)


def zonal_filter(values, rates):
    capacity, tile_rows, width = values.shape
    blocks = width // 128
    shaped = values.reshape(capacity, tile_rows, blocks, 128)
    log_decay = jnp.log1p(-rates)[:, :, None, None]
    gains = gain_of(rates)[:, :, None, None]
    offset = jnp.arange(128, dtype=jnp.float32)
    rising = jnp.exp(offset * log_decay)
    falling = jnp.exp(-offset * log_decay)
    index = jnp.arange(128)
    upto = (index[:, None] <= index[None, :]).astype(jnp.float32)
    block_decay = jnp.exp(128.0 * log_decay[..., 0])
    partial_value = jnp.einsum(
        "crbj,ji->crbi", shaped * gains * falling, upto, precision=HIGHEST_PRECISION
    )
    local = rising * partial_value
    entering = carry_blocks(block_decay, local[..., 127])
    forward = local + rising * jnp.exp(log_decay) * entering[..., None]
    partial_back = jnp.einsum(
        "crbj,ij->crbi", forward * gains * rising, upto, precision=HIGHEST_PRECISION
    )
    local_back = falling * partial_back
    from_above = jnp.flip(carry_blocks(block_decay, jnp.flip(local_back[..., 0], 2)), 2)
    backward = local_back + jnp.exp((128.0 - offset) * log_decay) * from_above[..., None]
    return backward.reshape(capacity, tile_rows, width)


def column_filter(values, rates):
    capacity, rows, cols = values.shape
    block = min(rows, 128)
    blocks = rows // block
    shaped = values.reshape(capacity, blocks, block, cols)
    log_decay = jnp.log1p(-rates).reshape(capacity, blocks, block)
    gains = gain_of(rates).reshape(capacity, blocks, block)
    forward_mat, backward_mat = chain_matrices(log_decay, gains)
    local = jnp.einsum("cbij,cbjx->cbix", forward_mat, shaped, precision=HIGHEST_PRECISION)
    inclusive = jnp.cumsum(log_decay, axis=2)
    whole_decay = inclusive[:, :, -1]
    block_decay = jnp.exp(whole_decay)
    entering = carry_row_blocks(block_decay, local[:, :, -1, :])
    forward = local + jnp.exp(inclusive)[..., None] * entering[:, :, None, :]
    local_back = jnp.einsum("cbij,cbjx->cbix", backward_mat, forward, precision=HIGHEST_PRECISION)
    from_above = jnp.flip(
        carry_row_blocks(jnp.flip(block_decay, 1), jnp.flip(local_back[:, :, 0, :], 1)), 1
    )
    exclusive = inclusive - log_decay
    tail = jnp.exp(whole_decay[..., None] - exclusive)
    backward = local_back + tail[..., None] * from_above[:, :, None, :]
    return backward.reshape(capacity, rows, cols)


def shards(increment, vert_rate, zonal_rate, merid_rate, lat_band, slab_owner):
    slabs, tile_rows, tile_cols = increment.shape
    groups_x = lax.axis_size("tx")
    capacity = 2 * slabs // groups_x
    index_x = lax.axis_index("tx")
    index_y = lax.axis_index("ty")
    vert_fwd, vert_bwd = chain_matrices(jnp.log1p(-vert_rate), gain_of(vert_rate))
    vert_matrix = jnp.einsum("vij,vjk->vik", vert_bwd, vert_fwd, precision=HIGHEST_PRECISION)
    vertical = vertical_apply(vert_matrix, increment)
    slab_index = jnp.arange(slabs, dtype=jnp.int32)
    same = slab_owner[:, None] == slab_owner[None, :]
    earlier = slab_index[None, :] < slab_index[:, None]
    slot = jnp.sum(jnp.logical_and(same, earlier), axis=1)
    target = slab_owner * capacity + slot
    slot_rows = jnp.arange(groups_x * capacity, dtype=jnp.int32)
    matches = target[None, :] == slot_rows[:, None]
    source = jnp.sum(jnp.where(matches, slab_index[None, :], 0), axis=1)
    filled = jnp.any(matches, axis=1).astype(jnp.float32)
    outgoing = jnp.take(vertical, source, axis=0) * filled[:, None, None]
    lines = lax.all_to_all(outgoing, "tx", split_axis=0, concat_axis=2, tiled=True)
    mine = lax.dynamic_slice_in_dim(source, index_x * capacity, capacity)
    mine_filled = lax.dynamic_slice_in_dim(filled, index_x * capacity, capacity)
    slab_onehot = (mine[:, None] == slab_index[None, :]).astype(jnp.float32) * mine_filled[:, None]
    band_onehot = (lat_band[:, None] == jnp.arange(NBANDS)[None, :]).astype(jnp.float32)
    row_onehot = lax.dynamic_slice_in_dim(band_onehot, index_y * tile_rows, tile_rows)
    zonal_table = jnp.dot(slab_onehot, zonal_rate.T, precision=HIGHEST_PRECISION)
    merid_table = jnp.dot(slab_onehot, merid_rate.T, precision=HIGHEST_PRECISION)
    zonal_rows = jnp.dot(zonal_table, row_onehot.T, precision=HIGHEST_PRECISION)
    zonal = zonal_filter(lines, zonal_rows)
    columns = lax.all_to_all(zonal, "ty", split_axis=2, concat_axis=1, tiled=True)
    merid_full = jnp.dot(merid_table, band_onehot.T, precision=HIGHEST_PRECISION)
    smoothed_columns = column_filter(columns, merid_full)
    smoothed = lax.all_to_all(smoothed_columns, "ty", split_axis=1, concat_axis=2, tiled=True)
    returned = lax.all_to_all(smoothed, "tx", split_axis=2, concat_axis=0, tiled=True)
    gathered = jnp.take(returned, target, axis=0)
    covariance_product = vertical_apply(vert_matrix, gathered)
    return (covariance_product, smoothed)


def solution(mesh):
    return jax.shard_map(
        shards,
        mesh=mesh,
        in_specs=(P(None, "ty", "tx"), P(), P(), P(), P(), P()),
        out_specs=(P(None, "ty", "tx"), P("tx", "ty", None)),
        check_vma=False,
    )
```

profile of v0, /device:TPU:1, one launch (start us, length us, event | category | flops | bytes accessed | tf_op | source)
XLA Modules:
  0.0 487.3 jit_solution(7366706735983362756)
XLA Ops:
  0.6 0.9 convert_reduce_fusion
  1.6 0.7 compare_and_fusion.1
  2.5 0.7 negate_log-plus-one_fusion.1
  3.1 0.2 reduce_window_sum.24
  3.3 0.7 fusion.108
  4.0 1.7 reshape.152
  5.8 0.2 fusion.61
  6.0 1.8 fusion.118
  7.8 0.4 copy.268
  8.2 2.7 gather_fusion
  10.9 4.4 select_multiply_fusion
  15.3 6.3 %all-to-all-start = ((f32[64,40,384]{2,1,0:T(8,128)}), f32[64,40,384]{2,1,0:T(8,128)}, u32[]{:S(2)}, u32[]{:S(2)}) async-start(f32[64,40,384]{2,1,0:T(8,128)} %select_multiply_fusion), calls=%async_computation | async-start | bytes 7864320 | tf_op jit(solution)/shard_map/all_to_all | solution.py:123
  21.8 0.2 fusion.87
  22.0 0.2 iota_compare_fusion
  22.2 0.2 fusion.111
  22.4 0.2 multiply_exponential_fusion
  22.5 45.0 %all-to-all-done = f32[64,40,384]{2,1,0:T(8,128)} async-done(((f32[64,40,384]{2,1,0:T(8,128)}), f32[64,40,384]{2,1,0:T(8,128)}, u32[]{:S(2)}, u32[]{:S(2)}) %all-to-all-start) | async-done | bytes 3932192 | tf_op jit(solution)/shard_map/all_to_all | solution.py:123
  67.6 6.3 %copy.226 = f32[8,40,8,384]{3,2,1,0:T(8,128)} copy(f32[8,40,8,384]{3,1,0,2:T(8,128)} %bitcast.5) | data formatting | bytes 7864320 | tf_op jit(solution)/shard_map/all_to_all | solution.py:123
  73.9 4.7 reshape.154
  78.5 4.4 fusion.22
  82.9 1.9 copy-done.2
  84.8 2.9 slice.372
  87.8 3.0 copy.227
  91.9 0.1 copy.266
  92.1 5.7 %fusion.31 = f32[8,40,24,128]{3,2,1,0:T(8,128)} fusion(f32[8,40,24,128]{3,2,1,0:T(8,128)} %copy-done.2, f32[8,40,24]{2,1,0:T(8,128)S(1)} %concatenate.46.clone, f32[8,40,128]{2,1,0:T(8,128)S(1)} %get-tuple-element.29, f32[8,40]{1,0:T(8,128)S(1)} %get-tuple-element.37, f32[8,40,128]{2,1,0:T(8,128)S(1)} %get-tuple-element.30, ...), kind=kOutput, calls=%fused_computation.34 | convolution fusion | flops 1514881024 | bytes 8387840 | tf_op jit(solution)/shard_map/crbj,ij->crbi/dot_general | solution.py:71
  97.8 3.0 copy.231
  102.1 4.1 multiply_add_fusion.1
  106.2 7.9 %copy.260 = f32[8,40,24,128]{1,0,3,2:T(8,128)} copy(f32[8,40,24,128]{3,2,1,0:T(8,128)} %multiply_add_fusion.1) | data formatting | bytes 7864320 | tf_op jit(solution)/shard_map/reshape | solution.py:77
  114.1 17.2 %reshape.179 = f32[16,1,61440]{2,1,0:T(1,128)} reshape(f32[3072,8,40]{2,1,0:T(8,128)} %bitcast.74) | data formatting | bytes 7864320
  131.2 8.2 %all-to-all-start.1 = ((f32[16,1,61440]{2,1,0:T(1,128)}), f32[16,1,61440]{2,1,0:T(1,128)}, u32[]{:S(2)}, u32[]{:S(2)}) async-start(f32[16,1,61440]{2,1,0:T(1,128)} %reshape.179), calls=%async_computation.1 | async-start | bytes 7864320 | tf_op jit(solution)/shard_map/all_to_all | solution.py:133
  139.4 0.2 fusion.89
  139.6 0.4 fusion.100
  140.0 1.4 reduce_window_sum.25
  141.6 0.1 copy.240
  142.1 0.1 copy.244
  143.1 0.2 slice_reduce_fusion.1
  143.3 0.2 slice_reduce_fusion
  143.5 53.7 %all-to-all-done.1 = f32[16,1,61440]{2,1,0:T(1,128)} async-done(((f32[16,1,61440]{2,1,0:T(1,128)}), f32[16,1,61440]{2,1,0:T(1,128)}, u32[]{:S(2)}, u32[]{:S(2)}) %all-to-all-start.1) | async-done | bytes 3932192 | tf_op jit(solution)/shard_map/all_to_all | solution.py:133
  197.2 0.5 broadcast.205
  197.7 13.6 %reduce.4 = f32[16,61440]{1,0:T(8,128)} reduce(f32[16,1,61440]{2,1,0:T(1,128)} %all-to-all-done.1, f32[]{:T(128)} %broadcast.205), dimensions={1}, to_apply=%all_to_all.51.reduce_sub_computation | reduce | bytes 7864324 | tf_op jit(solution)/shard_map/all_to_all | solution.py:133
  211.4 18.7 %reshape.180 = f32[3072,8,40]{2,1,0:T(8,128)} reshape(f32[16,61440]{1,0:T(8,128)} %reduce.4) | data formatting | bytes 7864320
  230.0 10.9 %copy.236 = f32[8,40,16,192]{3,1,2,0:T(8,128)} copy(f32[8,40,16,192]{1,0,3,2:T(8,128)} %bitcast.75) | data formatting | bytes 7864320 | tf_op jit(solution)/shard_map/all_to_all | solution.py:133
  240.9 11.2 %fusion.11 = f32[8,5,128,192]{2,3,1,0:T(8,128)S(1)} fusion(f32[8,5,128,192]{3,2,1,0:T(8,128)} %bitcast.82, f32[8,5,128]{2,1,0:T(8,128)S(1)} %copy.224, f32[8,5,128]{2,1,0:T(8,128)S(1)} %copy.223, pred[128,128]{1,0:T(8,128)(4,1)S(1)} %iota_compare_fusion.1), kind=kOutput, calls=%fused_computation.16 | convolution fusion | flops 1512570880 | bytes 7921664 | tf_op jit(solution)/shard_map/cbij,cbjx->cbix/dot_general | solution.py:88
  252.1 1.9 copy-done.3
  254.0 2.9 slice.398
  257.0 3.5 copy.239
  260.8 9.1 %fusion = f32[8,5,128,192]{2,3,1,0:T(8,128)} fusion(f32[8,5,128,192]{2,3,1,0:T(8,128)} %copy-done.3, f32[8,5,192]{2,1,0:T(8,128)S(1)} %concatenate.53.clone, f32[8,5,128]{2,1,0:T(8,128)S(1)} %copy.238, f32[8,5,128]{2,1,0:T(8,128)S(1)} %copy.223, f32[8,5,128]{2,1,0:T(8,128)S(1)} %copy.221, pred[128,128]{1,0:T(8,128)(4,1)S(1)} %iota_compare_fusion.2), kind=kOutput, calls=%fused_computation.3 | convolution fusion | flops 1514536960 | bytes 7972864 | tf_op jit(solution)/shard_map/cbij,cbjx->cbix/dot_general | solution.py:94
  269.9 3.5 copy.247
  273.8 4.1 multiply_add_fusion
  277.9 5.9 %copy.262 = f32[8,5,128,192]{3,0,2,1:T(8,128)} copy(f32[8,5,128,192]{2,3,1,0:T(8,128)} %multiply_add_fusion) | data formatting | bytes 7864320 | tf_op jit(solution)/shard_map/reshape | solution.py:101
  283.8 65.7 %all_to_all.66 = f32[8,640,192]{2,0,1:T(8,128)S(1)} all-to-all(f32[8,640,192]{2,0,1:T(8,128)} %bitcast.80), channel_id=1, replica_groups=mesh['tx'=8,'ty'=16] {'ty'}, dimensions={1} | all-to-all | bytes 7864320 | tf_op jit(solution)/shard_map/all_to_all | solution.py:136
  349.5 5.3 %copy.254 = f32[8,40,16,192]{3,2,1,0:T(8,128)} copy(f32[8,40,16,192]{3,0,1,2:T(8,128)S(1)} %bitcast.81) | data formatting | bytes 7864320 | tf_op jit(solution)/shard_map/all_to_all | solution.py:136
  354.8 5.8 %all_to_all.57 = f32[8,40,3072]{2,1,0:T(8,128)} reshape(f32[8,40,16,192]{3,2,1,0:T(8,128)} %copy.254) | data formatting | bytes 7864320 | tf_op jit(solution)/shard_map/all_to_all | solution.py:136
  360.6 8.8 %copy.255 = f32[8,40,3072]{1,0,2:T(8,128)} copy(f32[8,40,3072]{2,1,0:T(8,128)} %all_to_all.57) | data formatting | bytes 7864320 | tf_op jit(solution)/shard_map/all_to_all | solution.py:136
  369.5 14.8 %reshape.181 = f32[8,1,122880]{2,1,0:T(1,128)} reshape(f32[3072,8,40]{2,1,0:T(8,128)} %bitcast.77) | data formatting | bytes 7864320
  384.3 7.9 %all-to-all-start.3 = ((f32[8,1,122880]{2,1,0:T(1,128)}), f32[8,1,122880]{2,1,0:T(1,128)}, u32[]{:S(2)}, u32[]{:S(2)}) async-start(f32[8,1,122880]{2,1,0:T(1,128)} %reshape.181), calls=%async_computation.3 | async-start | bytes 7864320 | tf_op jit(solution)/shard_map/all_to_all | solution.py:137
  392.2 45.8 %all-to-all-done.3 = f32[8,1,122880]{2,1,0:T(1,128)} async-done(((f32[8,1,122880]{2,1,0:T(1,128)}), f32[8,1,122880]{2,1,0:T(1,128)}, u32[]{:S(2)}, u32[]{:S(2)}) %all-to-all-start.3) | async-done | bytes 3932192 | tf_op jit(solution)/shard_map/all_to_all | solution.py:137
  438.1 13.9 %reduce.5 = f32[8,122880]{1,0:T(8,128)} reduce(f32[8,1,122880]{2,1,0:T(1,128)} %all-to-all-done.3, f32[]{:T(128)} %broadcast.205), dimensions={1}, to_apply=%all_to_all.58.reduce_sub_computation | reduce | bytes 7864324 | tf_op jit(solution)/shard_map/all_to_all | solution.py:137
  452.0 16.8 %reshape.182 = f32[3072,8,40]{2,1,0:T(8,128)} reshape(f32[8,122880]{1,0:T(8,128)} %reduce.5) | data formatting | bytes 7864320
  468.7 9.1 %copy.257 = f32[8,8,40,384]{3,2,1,0:T(8,128)} copy(f32[8,8,40,384]{2,1,3,0:T(8,128)} %bitcast.76) | data formatting | bytes 7864320 | tf_op jit(solution)/shard_map/all_to_all | solution.py:137
  477.8 4.1 gather_fusion.1
  481.9 1.7 gather.12
  483.6 1.8 fusion.25
  485.4 1.6 copy.269
  (147 shorter events, 4.6 us)
Async XLA Ops:
  0.6 21.2 %copy-start = (f32[16,32]{1,0:T(8,128)S(1)}, f32[16,32]{1,0:T(8,128)}, u32[]{:S(2)}) copy-start(f32[16,32]{1,0:T(8,128)} %param.8) | copy-start | bytes 6148
  15.3 6.7 %copy-start.4 = (s32[640]{0:T(1024)S(1)}, s32[640]{0:T(1024)}, u32[]{:S(2)}) copy-start(s32[640]{0:T(1024)} %param.10) | copy-start | bytes 7684
  15.3 52.2 %all-to-all-start = ((f32[64,40,384]{2,1,0:T(8,128)}), f32[64,40,384]{2,1,0:T(8,128)}, u32[]{:S(2)}, u32[]{:S(2)}) async-start(f32[64,40,384]{2,1,0:T(8,128)} %select_multiply_fusion), calls=%async_computation | async-start | bytes 7864320 | tf_op jit(solution)/shard_map/all_to_all | solution.py:123
  82.9 1.9 copy-start.2
  131.2 8.2 %copy-start.5 = (f32[16,32]{1,0:T(8,128)S(1)}, f32[16,32]{1,0:T(8,128)}, u32[]{:S(2)}) copy-start(f32[16,32]{1,0:T(8,128)} %param.9) | copy-start | bytes 6148
  131.2 66.0 %all-to-all-start.1 = ((f32[16,1,61440]{2,1,0:T(1,128)}), f32[16,1,61440]{2,1,0:T(1,128)}, u32[]{:S(2)}, u32[]{:S(2)}) async-start(f32[16,1,61440]{2,1,0:T(1,128)} %reshape.179), calls=%async_computation.1 | async-start | bytes 7864320 | tf_op jit(solution)/shard_map/all_to_all | solution.py:133
  252.1 1.9 copy-start.3
  384.3 53.8 %all-to-all-start.3 = ((f32[8,1,122880]{2,1,0:T(1,128)}), f32[8,1,122880]{2,1,0:T(1,128)}, u32[]{:S(2)}, u32[]{:S(2)}) async-start(f32[8,1,122880]{2,1,0:T(1,128)} %reshape.181), calls=%async_computation.3 | async-start | bytes 7864320 | tf_op jit(solution)/shard_map/all_to_all | solution.py:137
  481.9 5.2 %copy-start.1 = (f32[16,32]{1,0:T(8,128)S(1)}, f32[16,32]{1,0:T(8,128)}, u32[]{:S(2)}) copy-start(f32[16,32]{1,0:T(8,128)} %param.8) | copy-start | bytes 6148
where the time goes:
time: 493 us; the launch traced here: 487 us
  local copies, waits for them, and re-layouts  172 us (35%)
  waiting for transfers between devices  145 us (29%)
  blocking collectives  65.7 us (13%)
  other arithmetic  46.2 us (9%)
  matrix products  35 us (7%)
  starting transfers between devices  22.4 us (5%)
    unnamed x24, local copies, waits for them, and re-layouts  73.5 us
    all_to_all x1, blocking collectives, shards(): lax.all_to_all(smoothed_columns, 'ty', split_axis=1, concat_axis=2, tiled...  65.7 us
    all_to_all x1, waiting for transfers between devices, shards(): lax.all_to_all(zonal, 'ty', split_axis=2, concat_axis=1, tiled=True)  53.7 us
    all_to_all x1, waiting for transfers between devices, shards(): lax.all_to_all(smoothed, 'tx', split_axis=2, concat_axis=0, tiled=True)  45.8 us
    all_to_all x1, waiting for transfers between devices, shards(): lax.all_to_all(outgoing, 'tx', split_axis=0, concat_axis=2, tiled=True)  45 us
    all_to_all x3, local copies, waits for them, and re-layouts, shards(): lax.all_to_all(smoothed_columns, 'ty', split_axis=1, concat_axis=2, tiled...  20 us
    all_to_all x1, other arithmetic, shards(): lax.all_to_all(smoothed, 'tx', split_axis=2, concat_axis=0, tiled=True)  13.9 us
    all_to_all x1, other arithmetic, shards(): lax.all_to_all(zonal, 'ty', split_axis=2, concat_axis=1, tiled=True)  13.6 us
  transfers between devices with their start and end apart: 3, of which 3 were waited for; matrix products, arithmetic and copies ran while one was open for 1% of the time, Pallas kernels for 0%

commit v1 on v0

--- a/solution.py
+++ b/solution.py
@@ -134,7 +134,10 @@
     merid_full = jnp.dot(merid_table, band_onehot.T, precision=HIGHEST_PRECISION)
     smoothed_columns = column_filter(columns, merid_full)
     smoothed = lax.all_to_all(smoothed_columns, "ty", split_axis=1, concat_axis=2, tiled=True)
-    returned = lax.all_to_all(smoothed, "tx", split_axis=2, concat_axis=0, tiled=True)
+    count = lax.axis_size("tx")
+    pieces = jnp.stack(jnp.split(smoothed, count, axis=2), axis=0)
+    pieces = lax.all_to_all(pieces, "tx", split_axis=0, concat_axis=0)
+    returned = jnp.concatenate(pieces, axis=0)
     gathered = jnp.take(returned, target, axis=0)
     covariance_product = vertical_apply(vert_matrix, gathered)
     return (covariance_product, smoothed)

time: 493 us -> 444 us (0.901)
  local copies, waits for them, and re-layouts: 172 us -> 137 us
  other arithmetic: 46.2 us -> 32.3 us
    unnamed x24 -> x29, local copies, waits for them, and re-layouts: 73.5 us -> 54.9 us
    all_to_all x1 -> x0, other arithmetic: 13.9 us -> none  [shards(): lax.all_to_all(smoothed, 'tx', split_axis=2, concat_axis=0, tiled=True)]
    all_to_all x1 -> x0, local copies, waits for them, and re-layouts: 9.1 us -> none  [shards(): lax.all_to_all(smoothed, 'tx', split_axis=2, concat_axis=0, tiled=True)]
    all_to_all x3 -> x2, local copies, waits for them, and re-layouts: 20 us -> 11.1 us  [shards(): lax.all_to_all(smoothed_columns, 'ty', split_axis=1, concat_axis=2, tiled...]
where the time goes in v1:
time: 444 us; the launch traced here: 439 us
  waiting for transfers between devices  145 us (33%)
  local copies, waits for them, and re-layouts  137 us (31%)
  blocking collectives  65.7 us (15%)
  matrix products  35.1 us (8%)
  other arithmetic  32.3 us (7%)
  starting transfers between devices  22.5 us (5%)
    all_to_all x1, blocking collectives, shards(): lax.all_to_all(smoothed_columns, 'ty', split_axis=1, concat_axis=2, tiled...  65.7 us
    unnamed x29, local copies, waits for them, and re-layouts  54.9 us
    all_to_all x1, waiting for transfers between devices, shards(): lax.all_to_all(zonal, 'ty', split_axis=2, concat_axis=1, tiled=True)  53.7 us
    all_to_all x1, waiting for transfers between devices, shards(): pieces = lax.all_to_all(pieces, 'tx', split_axis=0, concat_axis=0)  45.8 us
    all_to_all x1, waiting for transfers between devices, shards(): lax.all_to_all(outgoing, 'tx', split_axis=0, concat_axis=2, tiled=True)  45 us
    all_to_all x1, other arithmetic, shards(): lax.all_to_all(zonal, 'ty', split_axis=2, concat_axis=1, tiled=True)  13.6 us
    all_to_all x2, local copies, waits for them, and re-layouts, shards(): lax.all_to_all(zonal, 'ty', split_axis=2, concat_axis=1, tiled=True)  11.4 us
    dot_general x1, matrix products, column_filter(): jnp.einsum('cbij,cbjx->cbix', forward_mat, shaped, precision=HIGHEST_PREC...  11.2 us
  transfers between devices with their start and end apart: 3, of which 3 were waited for; matrix products, arithmetic and copies ran while one was open for 1% of the time, Pallas kernels for 0%

profile of v1, /device:TPU:1, one launch (start us, length us, event | category | flops | bytes accessed | tf_op | source)
XLA Modules:
  0.0 438.8 jit_solution(17386085900638693960)
XLA Ops:
  0.6 0.9 convert_reduce_fusion
  1.6 0.7 compare_and_fusion.1
  2.5 0.7 negate_log-plus-one_fusion.1
  3.1 0.2 reduce_window_sum.24
  3.3 0.7 fusion.116
  4.0 1.7 reshape.155
  5.8 0.2 fusion.69
  6.0 1.8 fusion.126
  7.8 0.4 copy.250
  8.2 2.7 gather_fusion
  10.9 4.4 %select_multiply_fusion = f32[64,40,384]{2,1,0:T(8,128)} fusion(f32[64,40,384]{2,1,0:T(8,128)} %gather_fusion, f32[64]{0:T(128)S(1)} %convert_element_type.14, pred[64]{0:T(512)(128)(4,1)S(1)} %compare_and_fusion), kind=kLoop, calls=%fused_computation.15 | loop fusion | flops 1966080 | bytes 7864640 | tf_op jit(solution)/shard_map/mul | solution.py:122
  15.3 6.7 %all-to-all-start = ((f32[64,40,384]{2,1,0:T(8,128)}), f32[64,40,384]{2,1,0:T(8,128)}, u32[]{:S(2)}, u32[]{:S(2)}) async-start(f32[64,40,384]{2,1,0:T(8,128)} %select_multiply_fusion), calls=%async_computation | async-start | bytes 7864320 | tf_op jit(solution)/shard_map/all_to_all | solution.py:123
  22.2 0.2 fusion.95
  22.4 0.2 iota_compare_fusion
  22.5 0.2 fusion.119
  22.7 0.2 multiply_exponential_fusion
  22.9 45.0 %all-to-all-done = f32[64,40,384]{2,1,0:T(8,128)} async-done(((f32[64,40,384]{2,1,0:T(8,128)}), f32[64,40,384]{2,1,0:T(8,128)}, u32[]{:S(2)}, u32[]{:S(2)}) %all-to-all-start) | async-done | bytes 3932192 | tf_op jit(solution)/shard_map/all_to_all | solution.py:123
  67.9 6.3 %copy.213 = f32[8,40,8,384]{3,2,1,0:T(8,128)} copy(f32[8,40,8,384]{3,1,0,2:T(8,128)} %bitcast.5) | data formatting | bytes 7864320 | tf_op jit(solution)/shard_map/all_to_all | solution.py:123
  74.2 4.7 %reshape.157 = f32[8,40,24,128]{3,2,1,0:T(8,128)} reshape(f32[8,40,8,384]{3,2,1,0:T(8,128)} %copy.213) | data formatting | bytes 7864320 | tf_op jit(solution)/shard_map/reshape | solution.py:56
  78.9 4.4 fusion.22
  83.3 1.9 copy-done.2
  85.2 2.9 slice.372
  88.1 3.0 copy.214
  92.4 5.7 %fusion.31 = f32[8,40,24,128]{3,2,1,0:T(8,128)} fusion(f32[8,40,24,128]{3,2,1,0:T(8,128)} %copy-done.2, f32[8,40,24]{2,1,0:T(8,128)S(1)} %concatenate.46.clone, f32[8,40,128]{2,1,0:T(8,128)S(1)} %get-tuple-element.29, f32[8,40]{1,0:T(8,128)S(1)} %get-tuple-element.37, f32[8,40,128]{2,1,0:T(8,128)S(1)} %get-tuple-element.30, ...), kind=kOutput, calls=%fused_computation.34 | convolution fusion | flops 1514881024 | bytes 8387840 | tf_op jit(solution)/shard_map/crbj,ij->crbi/dot_general | solution.py:71
  98.1 3.0 copy.218
  102.4 4.1 multiply_add_fusion.1
  106.5 7.9 %copy.244 = f32[8,40,24,128]{1,0,3,2:T(8,128)} copy(f32[8,40,24,128]{3,2,1,0:T(8,128)} %multiply_add_fusion.1) | data formatting | bytes 7864320 | tf_op jit(solution)/shard_map/reshape | solution.py:77
  114.4 17.2 %reshape.183 = f32[16,1,61440]{2,1,0:T(1,128)} reshape(f32[3072,8,40]{2,1,0:T(8,128)} %bitcast.100) | data formatting | bytes 7864320
  131.5 8.0 %all-to-all-start.1 = ((f32[16,1,61440]{2,1,0:T(1,128)}), f32[16,1,61440]{2,1,0:T(1,128)}, u32[]{:S(2)}, u32[]{:S(2)}) async-start(f32[16,1,61440]{2,1,0:T(1,128)} %reshape.183), calls=%async_computation.1 | async-start | bytes 7864320 | tf_op jit(solution)/shard_map/all_to_all | solution.py:133
  139.5 0.2 fusion.97
  139.7 0.4 fusion.108
  140.1 1.4 reduce_window_sum.25
  143.2 0.2 slice_reduce_fusion.1
  143.4 0.2 slice_reduce_fusion
  143.6 53.7 %all-to-all-done.1 = f32[16,1,61440]{2,1,0:T(1,128)} async-done(((f32[16,1,61440]{2,1,0:T(1,128)}), f32[16,1,61440]{2,1,0:T(1,128)}, u32[]{:S(2)}, u32[]{:S(2)}) %all-to-all-start.1) | async-done | bytes 3932192 | tf_op jit(solution)/shard_map/all_to_all | solution.py:133
  197.3 0.5 broadcast.205
  197.8 13.6 %reduce.4 = f32[16,61440]{1,0:T(8,128)} reduce(f32[16,1,61440]{2,1,0:T(1,128)} %all-to-all-done.1, f32[]{:T(128)} %broadcast.205), dimensions={1}, to_apply=%all_to_all.41.reduce_sub_computation | reduce | bytes 7864324 | tf_op jit(solution)/shard_map/all_to_all | solution.py:133
  211.4 18.7 %reshape.184 = f32[3072,8,40]{2,1,0:T(8,128)} reshape(f32[16,61440]{1,0:T(8,128)} %reduce.4) | data formatting | bytes 7864320
  230.1 10.9 %copy.223 = f32[8,40,16,192]{3,1,2,0:T(8,128)} copy(f32[8,40,16,192]{1,0,3,2:T(8,128)} %bitcast.101) | data formatting | bytes 7864320 | tf_op jit(solution)/shard_map/all_to_all | solution.py:133
  241.0 11.2 %fusion.11 = f32[8,5,128,192]{2,3,1,0:T(8,128)S(1)} fusion(f32[8,5,128,192]{3,2,1,0:T(8,128)} %bitcast.106, f32[8,5,128]{2,1,0:T(8,128)S(1)} %copy.211, f32[8,5,128]{2,1,0:T(8,128)S(1)} %copy.210, pred[128,128]{1,0:T(8,128)(4,1)S(1)} %iota_compare_fusion.1), kind=kOutput, calls=%fused_computation.16 | convolution fusion | flops 1512570880 | bytes 7921664 | tf_op jit(solution)/shard_map/cbij,cbjx->cbix/dot_general | solution.py:88
  252.2 1.9 copy-done.3
  254.1 2.9 slice.398
  257.0 3.5 copy.226
  260.9 9.1 %fusion = f32[8,5,128,192]{2,3,1,0:T(8,128)} fusion(f32[8,5,128,192]{2,3,1,0:T(8,128)} %copy-done.3, f32[8,5,192]{2,1,0:T(8,128)S(1)} %concatenate.53.clone, f32[8,5,128]{2,1,0:T(8,128)S(1)} %copy.225, f32[8,5,128]{2,1,0:T(8,128)S(1)} %copy.210, f32[8,5,128]{2,1,0:T(8,128)S(1)} %copy.208, pred[128,128]{1,0:T(8,128)(4,1)S(1)} %iota_compare_fusion.2), kind=kOutput, calls=%fused_computation.3 | convolution fusion | flops 1514536960 | bytes 7972864 | tf_op jit(solution)/shard_map/cbij,cbjx->cbix/dot_general | solution.py:94
  270.0 3.5 copy.234
  273.9 4.1 multiply_add_fusion
  277.9 5.9 %copy.246 = f32[8,5,128,192]{3,0,2,1:T(8,128)} copy(f32[8,5,128,192]{2,3,1,0:T(8,128)} %multiply_add_fusion) | data formatting | bytes 7864320 | tf_op jit(solution)/shard_map/reshape | solution.py:101
  283.9 65.7 %all_to_all.53 = f32[8,640,192]{2,0,1:T(8,128)S(1)} all-to-all(f32[8,640,192]{2,0,1:T(8,128)} %bitcast.104), channel_id=1, replica_groups=mesh['tx'=8,'ty'=16] {'ty'}, dimensions={1} | all-to-all | bytes 7864320 | tf_op jit(solution)/shard_map/all_to_all | solution.py:136
  349.5 5.3 %copy.241 = f32[8,40,16,192]{3,2,1,0:T(8,128)} copy(f32[8,40,16,192]{3,0,1,2:T(8,128)S(1)} %bitcast.105) | data formatting | bytes 7864320 | tf_op jit(solution)/shard_map/all_to_all | solution.py:136
  354.9 5.8 %all_to_all.47 = f32[8,40,3072]{2,1,0:T(8,128)} reshape(f32[8,40,16,192]{3,2,1,0:T(8,128)} %copy.241) | data formatting | bytes 7864320 | tf_op jit(solution)/shard_map/all_to_all | solution.py:136
  360.7 1.8 fusion.57
  362.5 1.9 fusion.56
  364.4 1.8 fusion.55
  366.2 1.9 fusion.54
  368.1 1.8 fusion.53
  369.9 1.9 fusion.52
  371.8 1.8 fusion.51
  373.7 1.8 fusion.50
  375.5 7.9 %all-to-all-start.3 = ((f32[8,8,40,384]{3,2,1,0:T(8,128)}), f32[8,8,40,384]{3,2,1,0:T(8,128)}, u32[]{:S(2)}, u32[]{:S(2)}) async-start(f32[8,8,40,384]{3,2,1,0:T(8,128)} %fusion.50), calls=%async_computation.3 | async-start | bytes 7864320 | tf_op jit(solution)/shard_map/all_to_all | solution.py:139
  383.5 45.8 %all-to-all-done.3 = f32[8,8,40,384]{3,2,1,0:T(8,128)} async-done(((f32[8,8,40,384]{3,2,1,0:T(8,128)}), f32[8,8,40,384]{3,2,1,0:T(8,128)}, u32[]{:S(2)}, u32[]{:S(2)}) %all-to-all-start.3) | async-done | bytes 3932192 | tf_op jit(solution)/shard_map/all_to_all | solution.py:139
  429.3 4.1 gather_fusion.1
  433.4 1.7 gather.12
  435.1 1.8 fusion.25
  436.9 1.6 copy.251
  (150 shorter events, 5.0 us)
Async XLA Ops:
  0.6 21.5 %copy-start = (f32[16,32]{1,0:T(8,128)S(1)}, f32[16,32]{1,0:T(8,128)}, u32[]{:S(2)}) copy-start(f32[16,32]{1,0:T(8,128)} %param.8) | copy-start | bytes 6148
  15.3 7.0 %copy-start.4 = (s32[640]{0:T(1024)S(1)}, s32[640]{0:T(1024)}, u32[]{:S(2)}) copy-start(s32[640]{0:T(1024)} %param.10) | copy-start | bytes 7684
  15.3 52.6 %all-to-all-start = ((f32[64,40,384]{2,1,0:T(8,128)}), f32[64,40,384]{2,1,0:T(8,128)}, u32[]{:S(2)}, u32[]{:S(2)}) async-start(f32[64,40,384]{2,1,0:T(8,128)} %select_multiply_fusion), calls=%async_computation | async-start | bytes 7864320 | tf_op jit(solution)/shard_map/all_to_all | solution.py:123
  83.2 1.9 copy-start.2
  131.5 8.0 %copy-start.5 = (f32[16,32]{1,0:T(8,128)S(1)}, f32[16,32]{1,0:T(8,128)}, u32[]{:S(2)}) copy-start(f32[16,32]{1,0:T(8,128)} %param.9) | copy-start | bytes 6148
  131.5 65.8 %all-to-all-start.1 = ((f32[16,1,61440]{2,1,0:T(1,128)}), f32[16,1,61440]{2,1,0:T(1,128)}, u32[]{:S(2)}, u32[]{:S(2)}) async-start(f32[16,1,61440]{2,1,0:T(1,128)} %reshape.183), calls=%async_computation.1 | async-start | bytes 7864320 | tf_op jit(solution)/shard_map/all_to_all | solution.py:133
  252.2 1.9 copy-start.3
  375.5 53.8 %all-to-all-start.3 = ((f32[8,8,40,384]{3,2,1,0:T(8,128)}), f32[8,8,40,384]{3,2,1,0:T(8,128)}, u32[]{:S(2)}, u32[]{:S(2)}) async-start(f32[8,8,40,384]{3,2,1,0:T(8,128)} %fusion.50), calls=%async_computation.3 | async-start | bytes 7864320 | tf_op jit(solution)/shard_map/all_to_all | solution.py:139
  433.4 5.2 %copy-start.1 = (f32[16,32]{1,0:T(8,128)S(1)}, f32[16,32]{1,0:T(8,128)}, u32[]{:S(2)}) copy-start(f32[16,32]{1,0:T(8,128)} %param.8) | copy-start | bytes 6148
